TPU v7x, 256 devices: a whole 4x4x8 slice. The times are simulated.
256 devices in a mesh: mirror: 2 (over y_hi), slab: 64 (over z, y_lo, x), cols: 2 (over core).
Axes of the slice: x: 4, y: 4 (y_hi: 2, y_lo: 2; y = y_hi * 2 + y_lo), z: 8, core: 2. Of those that a mesh axis runs over, the one named last changes fastest.
Arguments:
- right_side: float32 [2, 1024, 65536], P('mirror', 'slab', 'cols'), parts along dimension 2, may hold values from -6 to 6
- analysis: float32 [2, 1024, 1024], P('mirror'), may hold values from -0.1875 to 0.1875
- synthesis: float32 [2, 1024, 1024], P('mirror'), may hold values from -0.1875 to 0.1875
- negated_eigen: float32 [2, 1024], P('mirror'), may hold values from 0.25 to 4
- wave_square: float32 [65536], P(('cols', 'slab')), parts along dimension 0, may hold values from 0.25 to 4
Outputs:
- solution: float32 [2, 1024, 65536], P('mirror', 'slab', 'cols'), parts along dimension 2
There are 2 independent parts, one for each index of `cols`. A program takes and returns all parts, laid end to end along the dimension named above; an argument that names none is the same for every part. Nothing has to cross between parts.
All inputs are finite; a program needn't handle non-finite values.
Results may differ from a plain program's by a relative error of at most 0.0001.
Values sent between devices are 32-bit elements; how exact they have to be, the bound alone decides.
No kernel may reach another device: no remote copies, remote signals or barrier semaphores. Data moves between devices by JAX's collectives and lax.ppermute only.
A program may use at most 64 MiB of HBM per device.

v0:
```python
import jax
import jax.numpy as jnp
from jax import lax
from jax.sharding import PartitionSpec as P


def from_partner(value, axis, bit):
    mask = 2**bit
    pairs = [(source, source ^ mask) for source in range(lax.axis_size(axis))]
    return lax.ppermute(value, axis, pairs)


def mirror_swap(slab_piece):
    return from_partner(slab_piece, "mirror", 0)


def project(column_field, analysis, synthesis, negated_eigen, wave_square):
    coefficients = jnp.dot(
        analysis, column_field, precision=lax.Precision.HIGHEST, preferred_element_type=jnp.float32
    )
    scaled = coefficients / (negated_eigen[:, None] + wave_square[None, :])
    return -jnp.dot(
        synthesis, scaled, precision=lax.Precision.HIGHEST, preferred_element_type=jnp.float32
    )


def shards(right_side, analysis, synthesis, negated_eigen, wave_square):
    own_half = right_side[0]
    parity = lax.axis_index("mirror")
    parity_sign = (1 - 2 * parity).astype(jnp.float32)
    partner = mirror_swap(own_half)
    lower_half = jnp.where(parity == 0, own_half, partner)
    upper_half = jnp.where(parity == 0, partner, own_half)
    folded = (lower_half + parity_sign * upper_half) * 0.5
    columns = lax.all_to_all(folded, "slab", split_axis=1, concat_axis=0, tiled=True)
    solved = project(columns, analysis[0], synthesis[0], negated_eigen[0], wave_square)
    returned = lax.all_to_all(solved, "slab", split_axis=0, concat_axis=1, tiled=True)
    partner_back = mirror_swap(returned)
    even_part = jnp.where(parity == 0, returned, partner_back)
    odd_part = jnp.where(parity == 0, partner_back, returned)
    result = even_part + parity_sign * odd_part
    return result[None]


def solution(mesh):
    return jax.shard_map(
        shards,
        mesh=mesh,
        in_specs=(
            P("mirror", "slab", "cols"),
            P("mirror", None, None),
            P("mirror", None, None),
            P("mirror", None),
            P(("cols", "slab")),
        ),
        out_specs=P("mirror", "slab", "cols"),
        check_vma=False,
    )
```

profile of v0, /device:TPU:36, one launch (start us, length us, event | category | flops | bytes accessed | tf_op | source)
XLA Modules:
  0.0 242.4 jit_solution(17822131640532167315)
XLA Ops:
  0.0 3.2 %collective-permute-start = (f32[16,32768]{1,0:T(8,128)}, f32[16,32768]{1,0:T(8,128)S(1)}, u32[]{:S(2)}, u32[]{:S(2)}) collective-permute-start(f32[16,32768]{1,0:T(8,128)} %bitcast.39), channel_id=1, source_target_pairs={{0,128},{128,0},{1,129},{129,1},{2,130},{130,2},{3,131},{131,3},{4... | collective-permute-start | bytes 6291464 | tf_op jit(solution)/shard_map/ppermute | solution.py:10
  3.2 45.9 %collective-permute-done = f32[16,32768]{1,0:T(8,128)S(1)} collective-permute-done((f32[16,32768]{1,0:T(8,128)}, f32[16,32768]{1,0:T(8,128)S(1)}, u32[]{:S(2)}, u32[]{:S(2)}) %collective-permute-start) | collective-permute-done | bytes 2097184 | tf_op jit(solution)/shard_map/ppermute | solution.py:10
  49.1 1.9 add_multiply_fusion
  51.0 0.2 copy.17
  51.2 0.0 copy-start
  51.3 61.3 %all_to_all.38 = f32[16,64,512]{2,0,1:T(8,128)S(1)} all-to-all(f32[16,64,512]{2,0,1:T(8,128)S(1)} %bitcast.36), channel_id=1, replica_groups=mesh['mirror'=2,'slab'=64,'cols'=2] {'slab'}, dimensions={1} | all-to-all | bytes 4194304 | tf_op jit(solution)/shard_map/all_to_all | solution.py:35
  112.6 0.0 copy-done
  112.6 0.0 copy-start.1
  112.6 0.0 copy-start.2
  112.6 0.0 copy-start.3
  112.6 13.6 %fusion.2 = f32[512,1024]{1,0:T(8,128)S(1)} fusion(f32[1024,512]{1,0:T(8,128)S(1)} %bitcast.32, f32[1,1024,1024]{2,1,0:T(8,128)S(1)} %copy-done), kind=kOutput, calls=%fused_computation.2 | convolution fusion | flops 6442450944 | bytes 8388608 | tf_op jit(solution)/shard_map/dot_general | solution.py:18
  126.2 0.0 copy-done.1
  126.2 0.0 copy-done.2
  126.2 0.0 copy-done.3
  126.2 8.4 %negate_bitcast_fusion = f32[1024,512]{0,1:T(8,128)} fusion(f32[1,1024,1024]{2,1,0:T(8,128)S(1)} %copy-done.1, f32[512,1024]{1,0:T(8,128)S(1)} %fusion.2, f32[512]{0:T(512)S(1)} %copy-done.3, f32[1024]{0:T(1024)S(1)} %bitcast.40), kind=kOutput, calls=%fused_computation.7 | convolution fusion | flops 6444023808 | bytes 8394752 | tf_op jit(solution)/shard_map/dot_general | solution.py:22
  134.6 1.9 copy.12
  136.6 56.0 %all_to_all.39 = f32[64,16,512]{2,1,0:T(8,128)S(1)} all-to-all(f32[64,16,512]{2,1,0:T(8,128)S(1)} %bitcast.37), channel_id=1, replica_groups=mesh['mirror'=2,'slab'=64,'cols'=2] {'slab'}, dimensions={0} | all-to-all | bytes 4194304 | tf_op jit(solution)/shard_map/all_to_all | solution.py:37
  192.5 0.2 copy.15
  192.7 3.0 %collective-permute-start.1 = (f32[16,32768]{1,0:T(8,128)S(1)}, f32[16,32768]{1,0:T(8,128)S(1)}, u32[]{:S(2)}, u32[]{:S(2)}) collective-permute-start(f32[16,32768]{1,0:T(8,128)S(1)} %bitcast.33), channel_id=1, source_target_pairs={{0,128},{128,0},{1,129},{129,1},{2,130},{130,2},{3,131},{131,3},{4... | collective-permute-start | bytes 6291464 | tf_op jit(solution)/shard_map/ppermute | solution.py:10
  195.7 45.2 %collective-permute-done.1 = f32[16,32768]{1,0:T(8,128)S(1)} collective-permute-done((f32[16,32768]{1,0:T(8,128)S(1)}, f32[16,32768]{1,0:T(8,128)S(1)}, u32[]{:S(2)}, u32[]{:S(2)}) %collective-permute-start.1) | collective-permute-done | bytes 2097184 | tf_op jit(solution)/shard_map/ppermute | solution.py:10
  240.8 1.6 add_bitcast_fusion
Async XLA Ops:
  0.0 49.1 %collective-permute-start = (f32[16,32768]{1,0:T(8,128)}, f32[16,32768]{1,0:T(8,128)S(1)}, u32[]{:S(2)}, u32[]{:S(2)}) collective-permute-start(f32[16,32768]{1,0:T(8,128)} %bitcast.39), channel_id=1, source_target_pairs={{0,128},{128,0},{1,129},{129,1},{2,130},{130,2},{3,131},{131,3},{4... | collective-permute-start | bytes 6291464 | tf_op jit(solution)/shard_map/ppermute | solution.py:10
  51.2 61.3 %copy-start = (f32[1,1024,1024]{2,1,0:T(8,128)S(1)}, f32[1,1024,1024]{2,1,0:T(8,128)}, u32[]{:S(2)}) copy-start(f32[1,1024,1024]{2,1,0:T(8,128)} %param.6) | copy-start | bytes 12582916
  112.6 13.7 %copy-start.1 = (f32[1,1024,1024]{2,1,0:T(8,128)S(1)}, f32[1,1024,1024]{2,1,0:T(8,128)}, u32[]{:S(2)}) copy-start(f32[1,1024,1024]{2,1,0:T(8,128)} %param.7) | copy-start | bytes 12582916
  112.6 13.7 %copy-start.2 = (f32[1,1024]{1,0:T(1,128)S(1)}, f32[1,1024]{1,0:T(1,128)}, u32[]{:S(2)}) copy-start(f32[1,1024]{1,0:T(1,128)} %param.8) | copy-start | bytes 12292
  112.6 13.7 %copy-start.3 = (f32[512]{0:T(512)S(1)}, f32[512]{0:T(512)}, u32[]{:S(2)}) copy-start(f32[512]{0:T(512)} %param.9) | copy-start | bytes 6148
  192.7 48.1 %collective-permute-start.1 = (f32[16,32768]{1,0:T(8,128)S(1)}, f32[16,32768]{1,0:T(8,128)S(1)}, u32[]{:S(2)}, u32[]{:S(2)}) collective-permute-start(f32[16,32768]{1,0:T(8,128)S(1)} %bitcast.33), channel_id=1, source_target_pairs={{0,128},{128,0},{1,129},{129,1},{2,130},{130,2},{3,131},{131,3},{4... | collective-permute-start | bytes 6291464 | tf_op jit(solution)/shard_map/ppermute | solution.py:10
where the time goes:
time: 243 us; the launch traced here: 242 us
  blocking collectives  117 us (48%)
  waiting for transfers between devices  91 us (37%)
  matrix products  22 us (9%)
  starting transfers between devices  6.18 us (3%)
  other arithmetic  3.53 us (1%)
    ppermute x2, waiting for transfers between devices, from_partner(): return lax.ppermute(value, axis, pairs)  91 us
    all_to_all x1, blocking collectives, shards(): lax.all_to_all(folded, 'slab', split_axis=1, concat_axis=0, tiled=True)  61.3 us
    all_to_all x1, blocking collectives, shards(): lax.all_to_all(solved, 'slab', split_axis=0, concat_axis=1, tiled=True)  56 us
    dot_general x1, matrix products, project(): jnp.dot(analysis, column_field, precision=lax.Precision.HIGHEST, preferre...  13.6 us
    dot_general x1, matrix products, project(): jnp.dot(synthesis, scaled, precision=lax.Precision.HIGHEST, preferred_ele...  8.39 us
    ppermute x2, starting transfers between devices, from_partner(): return lax.ppermute(value, axis, pairs)  6.18 us
  transfers between devices with their start and end apart: 2, of which 2 were waited for; matrix products, arithmetic and copies ran while one was open for 0% of the time, Pallas kernels for 0%

commit v1 on v0

--- a/solution.py
+++ b/solution.py
@@ -34,7 +34,9 @@
     folded = (lower_half + parity_sign * upper_half) * 0.5
     columns = lax.all_to_all(folded, "slab", split_axis=1, concat_axis=0, tiled=True)
     solved = project(columns, analysis[0], synthesis[0], negated_eigen[0], wave_square)
-    returned = lax.all_to_all(solved, "slab", split_axis=0, concat_axis=1, tiled=True)
+    pieces = jnp.split(solved, lax.axis_size("slab"), axis=0)
+    received = lax.all_to_all(jnp.stack(pieces), "slab", 0, 0)
+    returned = jnp.concatenate(received, axis=1)
     partner_back = mirror_swap(returned)
     even_part = jnp.where(parity == 0, returned, partner_back)
     odd_part = jnp.where(parity == 0, partner_back, returned)

time: 243 us -> 366 us (1.51)
  local copies, waits for them, and re-layouts: 2.33 us -> 123 us
    another operation x0 -> x69, local copies, waits for them, and re-layouts: none -> 102 us  [shards(): received = lax.all_to_all(jnp.stack(pieces), 'slab', 0, 0)]
    unnamed x8 -> x137, local copies, waits for them, and re-layouts: 0.02 us -> 20.1 us
where the time goes in v1:
time: 366 us; the launch traced here: 362 us
  local copies, waits for them, and re-layouts  123 us (34%)
  blocking collectives  117 us (32%)
  waiting for transfers between devices  91 us (25%)
  matrix products  20.6 us (6%)
  starting transfers between devices  6.18 us (2%)
    another operation x69, local copies, waits for them, and re-layouts, shards(): received = lax.all_to_all(jnp.stack(pieces), 'slab', 0, 0)  102 us
    ppermute x2, waiting for transfers between devices, from_partner(): return lax.ppermute(value, axis, pairs)  91 us
    all_to_all x1, blocking collectives, shards(): lax.all_to_all(folded, 'slab', split_axis=1, concat_axis=0, tiled=True)  61.3 us
    all_to_all x1, blocking collectives, shards(): received = lax.all_to_all(jnp.stack(pieces), 'slab', 0, 0)  56 us
    unnamed x137, local copies, waits for them, and re-layouts  20.1 us
    dot_general x1, matrix products, project(): jnp.dot(analysis, column_field, precision=lax.Precision.HIGHEST, preferre...  13.5 us
  transfers between devices with their start and end apart: 2, of which 2 were waited for; matrix products, arithmetic and copies ran while one was open for 0% of the time, Pallas kernels for 0%

profile of v1, /device:TPU:36, one launch (start us, length us, event | category | flops | bytes accessed | tf_op | source)
XLA Modules:
  0.0 362.3 jit_solution(9721545643774538609)
XLA Ops:
  0.0 3.2 collective-permute-start
  3.2 45.9 %collective-permute-done = f32[16,32768]{1,0:T(8,128)S(1)} collective-permute-done((f32[16,32768]{1,0:T(8,128)}, f32[16,32768]{1,0:T(8,128)S(1)}, u32[]{:S(2)}, u32[]{:S(2)}) %collective-permute-start) | collective-permute-done | bytes 2097184 | tf_op jit(solution)/shard_map/ppermute | solution.py:10
  49.1 1.9 add_multiply_fusion
  51.3 61.3 %all_to_all.24 = f32[16,64,512]{2,0,1:T(8,128)S(1)} all-to-all(f32[16,64,512]{2,0,1:T(8,128)S(1)} %bitcast.163), channel_id=1, replica_groups=mesh['mirror'=2,'slab'=64,'cols'=2] {'slab'}, dimensions={1} | all-to-all | bytes 4194304 | tf_op jit(solution)/shard_map/all_to_all | solution.py:35
  112.6 13.5 %fusion.2 = f32[512,1024]{1,0:T(8,128)S(1)} fusion(f32[1024,512]{1,0:T(8,128)S(1)} %bitcast.159, f32[1,1024,1024]{2,1,0:T(8,128)S(1)} %copy-done), kind=kOutput, calls=%fused_computation.2 | convolution fusion | flops 6442450944 | bytes 8388608 | tf_op jit(solution)/shard_map/dot_general | solution.py:18
  126.1 7.1 %negate_bitcast_fusion = f32[1024,512]{0,1:T(8,128)S(1)} fusion(f32[1,1024,1024]{2,1,0:T(8,128)S(1)} %copy-done.34, f32[512,1024]{1,0:T(8,128)S(1)} %fusion.2, f32[512]{0:T(512)S(1)} %copy-done.36, f32[1024]{0:T(1024)S(1)} %bitcast.166), kind=kOutput, calls=%fused_computation.7 | convolution fusion | flops 6444023808 | bytes 8394752 | tf_op jit(solution)/shard_map/dot_general | solution.py:22
  133.6 3.4 slice_bitcast_fusion.38
  137.0 3.4 slice_bitcast_fusion
  140.4 3.0 slice_bitcast_fusion.19
  147.8 1.7 copy.107
  149.5 1.7 copy.106
  154.5 1.7 copy.103
  159.5 1.7 copy.100
  164.5 1.7 copy.97
  166.2 1.7 copy.96
  169.5 1.7 copy.94
  172.8 1.7 copy.92
  174.5 1.7 copy.91
  177.8 1.7 copy.89
  183.7 1.7 copy.141
  192.0 1.7 copy.136
  193.7 1.7 copy.135
  195.4 1.7 copy.134
  202.1 1.7 copy.130
  207.0 1.7 copy.127
  208.7 1.7 copy.126
  222.0 1.7 copy.118
  223.7 1.7 copy.117
  225.4 1.7 copy.116
  256.4 56.0 %all_to_all.25 = f32[64,16,512]{2,1,0:T(8,128)S(1)} all-to-all(f32[64,16,512]{2,1,0:T(8,128)S(1)} %constant_dynamic-update-slice_fusion), channel_id=1, replica_groups=mesh['mirror'=2,'slab'=64,'cols'=2] {'slab'}, dimensions={0} | all-to-all | bytes 4194304 | tf_op jit(solution)/shard_map/all_to_all | solution.py:38
  312.5 3.0 collective-permute-start.1
  315.5 45.2 %collective-permute-done.1 = f32[16,32768]{1,0:T(8,128)S(1)} collective-permute-done((f32[16,32768]{1,0:T(8,128)S(1)}, f32[16,32768]{1,0:T(8,128)S(1)}, u32[]{:S(2)}, u32[]{:S(2)}) %collective-permute-start.1) | collective-permute-done | bytes 2097184 | tf_op jit(solution)/shard_map/ppermute | solution.py:10
  (186 shorter events, 81.3 us)
Async XLA Ops:
  0.0 49.1 %collective-permute-start = (f32[16,32768]{1,0:T(8,128)}, f32[16,32768]{1,0:T(8,128)S(1)}, u32[]{:S(2)}, u32[]{:S(2)}) collective-permute-start(f32[16,32768]{1,0:T(8,128)} %bitcast.165), channel_id=1, source_target_pairs={{0,128},{128,0},{1,129},{129,1},{2,130},{130,2},{3,131},{131,3},{4... | collective-permute-start | bytes 6291464 | tf_op jit(solution)/shard_map/ppermute | solution.py:10
  51.2 61.3 %copy-start = (f32[1,1024,1024]{2,1,0:T(8,128)S(1)}, f32[1,1024,1024]{2,1,0:T(8,128)}, u32[]{:S(2)}) copy-start(f32[1,1024,1024]{2,1,0:T(8,128)} %param.6) | copy-start | bytes 12582916
  232.7 17.6 %copy-start.14 = (f32[1,16,512]{2,1,0:T(8,128)S(1)}, f32[1,16,512]{2,1,0:T(8,128)}, u32[]{:S(2)}) copy-start(f32[1,16,512]{2,1,0:T(8,128)} %copy.106) | copy-start | bytes 98308
  232.7 17.6 %copy-start.12 = (f32[1,16,512]{2,1,0:T(8,128)S(1)}, f32[1,16,512]{2,1,0:T(8,128)}, u32[]{:S(2)}) copy-start(f32[1,16,512]{2,1,0:T(8,128)} %copy.107) | copy-start | bytes 98308
  232.7 23.3 %copy-start.17 = (f32[1,16,512]{2,1,0:T(8,128)S(1)}, f32[1,16,512]{2,1,0:T(8,128)}, u32[]{:S(2)}) copy-start(f32[1,16,512]{2,1,0:T(8,128)} %copy.128) | copy-start | bytes 98308
  232.8 23.3 %copy-start.15 = (f32[1,16,512]{2,1,0:T(8,128)S(1)}, f32[1,16,512]{2,1,0:T(8,128)}, u32[]{:S(2)}) copy-start(f32[1,16,512]{2,1,0:T(8,128)} %copy.129) | copy-start | bytes 98308
  232.8 23.3 %copy-start.13 = (f32[1,16,512]{2,1,0:T(8,128)S(1)}, f32[1,16,512]{2,1,0:T(8,128)}, u32[]{:S(2)}) copy-start(f32[1,16,512]{2,1,0:T(8,128)} %copy.130) | copy-start | bytes 98308
  232.8 23.3 %copy-start.11 = (f32[1,16,512]{2,1,0:T(8,128)S(1)}, f32[1,16,512]{2,1,0:T(8,128)}, u32[]{:S(2)}) copy-start(f32[1,16,512]{2,1,0:T(8,128)} %copy.131) | copy-start | bytes 98308
  233.5 22.5 %copy-start.21 = (f32[1,16,512]{2,1,0:T(8,128)S(1)}, f32[1,16,512]{2,1,0:T(8,128)}, u32[]{:S(2)}) copy-start(f32[1,16,512]{2,1,0:T(8,128)} %copy.126) | copy-start | bytes 98308
  233.5 22.5 %copy-start.19 = (f32[1,16,512]{2,1,0:T(8,128)S(1)}, f32[1,16,512]{2,1,0:T(8,128)}, u32[]{:S(2)}) copy-start(f32[1,16,512]{2,1,0:T(8,128)} %copy.127) | copy-start | bytes 98308
  233.5 22.6 %copy-start.10 = (f32[1,16,512]{2,1,0:T(8,128)S(1)}, f32[1,16,512]{2,1,0:T(8,128)}, u32[]{:S(2)}) copy-start(f32[1,16,512]{2,1,0:T(8,128)} %copy.132) | copy-start | bytes 98308
  233.5 22.6 %copy-start.9 = (f32[1,16,512]{2,1,0:T(8,128)S(1)}, f32[1,16,512]{2,1,0:T(8,128)}, u32[]{:S(2)}) copy-start(f32[1,16,512]{2,1,0:T(8,128)} %copy.133) | copy-start | bytes 98308
  233.5 22.6 %copy-start.8 = (f32[1,16,512]{2,1,0:T(8,128)S(1)}, f32[1,16,512]{2,1,0:T(8,128)}, u32[]{:S(2)}) copy-start(f32[1,16,512]{2,1,0:T(8,128)} %copy.134) | copy-start | bytes 98308
  233.5 22.6 %copy-start.7 = (f32[1,16,512]{2,1,0:T(8,128)S(1)}, f32[1,16,512]{2,1,0:T(8,128)}, u32[]{:S(2)}) copy-start(f32[1,16,512]{2,1,0:T(8,128)} %copy.135) | copy-start | bytes 98308
  234.3 21.6 %copy-start.25 = (f32[1,16,512]{2,1,0:T(8,128)S(1)}, f32[1,16,512]{2,1,0:T(8,128)}, u32[]{:S(2)}) copy-start(f32[1,16,512]{2,1,0:T(8,128)} %copy.123) | copy-start | bytes 98308
  234.3 21.7 %copy-start.24 = (f32[1,16,512]{2,1,0:T(8,128)S(1)}, f32[1,16,512]{2,1,0:T(8,128)}, u32[]{:S(2)}) copy-start(f32[1,16,512]{2,1,0:T(8,128)} %copy.124) | copy-start | bytes 98308
  234.3 21.7 %copy-start.23 = (f32[1,16,512]{2,1,0:T(8,128)S(1)}, f32[1,16,512]{2,1,0:T(8,128)}, u32[]{:S(2)}) copy-start(f32[1,16,512]{2,1,0:T(8,128)} %copy.125) | copy-start | bytes 98308
  234.3 21.9 %copy-start.6 = (f32[1,16,512]{2,1,0:T(8,128)S(1)}, f32[1,16,512]{2,1,0:T(8,128)}, u32[]{:S(2)}) copy-start(f32[1,16,512]{2,1,0:T(8,128)} %copy.136) | copy-start | bytes 98308
  234.3 21.9 %copy-start.5 = (f32[1,16,512]{2,1,0:T(8,128)S(1)}, f32[1,16,512]{2,1,0:T(8,128)}, u32[]{:S(2)}) copy-start(f32[1,16,512]{2,1,0:T(8,128)} %copy.137) | copy-start | bytes 98308
  234.3 22.0 %copy-start.4 = (f32[1,16,512]{2,1,0:T(8,128)S(1)}, f32[1,16,512]{2,1,0:T(8,128)}, u32[]{:S(2)}) copy-start(f32[1,16,512]{2,1,0:T(8,128)} %copy.138) | copy-start | bytes 98308
  234.3 22.0 %copy-start.3 = (f32[1,16,512]{2,1,0:T(8,128)S(1)}, f32[1,16,512]{2,1,0:T(8,128)}, u32[]{:S(2)}) copy-start(f32[1,16,512]{2,1,0:T(8,128)} %copy.139) | copy-start | bytes 98308
  234.3 22.0 %copy-start.2 = (f32[1,16,512]{2,1,0:T(8,128)S(1)}, f32[1,16,512]{2,1,0:T(8,128)}, u32[]{:S(2)}) copy-start(f32[1,16,512]{2,1,0:T(8,128)} %copy.140) | copy-start | bytes 98308
  235.0 20.7 %copy-start.32 = (f32[1,16,512]{2,1,0:T(8,128)S(1)}, f32[1,16,512]{2,1,0:T(8,128)}, u32[]{:S(2)}) copy-start(f32[1,16,512]{2,1,0:T(8,128)} %copy.116) | copy-start | bytes 98308
  235.0 20.7 %copy-start.31 = (f32[1,16,512]{2,1,0:T(8,128)S(1)}, f32[1,16,512]{2,1,0:T(8,128)}, u32[]{:S(2)}) copy-start(f32[1,16,512]{2,1,0:T(8,128)} %copy.117) | copy-start | bytes 98308
  235.0 20.7 %copy-start.30 = (f32[1,16,512]{2,1,0:T(8,128)S(1)}, f32[1,16,512]{2,1,0:T(8,128)}, u32[]{:S(2)}) copy-start(f32[1,16,512]{2,1,0:T(8,128)} %copy.118) | copy-start | bytes 98308
  235.0 20.8 %copy-start.29 = (f32[1,16,512]{2,1,0:T(8,128)S(1)}, f32[1,16,512]{2,1,0:T(8,128)}, u32[]{:S(2)}) copy-start(f32[1,16,512]{2,1,0:T(8,128)} %copy.119) | copy-start | bytes 98308
  235.0 20.8 %copy-start.28 = (f32[1,16,512]{2,1,0:T(8,128)S(1)}, f32[1,16,512]{2,1,0:T(8,128)}, u32[]{:S(2)}) copy-start(f32[1,16,512]{2,1,0:T(8,128)} %copy.120) | copy-start | bytes 98308
  235.1 20.8 %copy-start.27 = (f32[1,16,512]{2,1,0:T(8,128)S(1)}, f32[1,16,512]{2,1,0:T(8,128)}, u32[]{:S(2)}) copy-start(f32[1,16,512]{2,1,0:T(8,128)} %copy.121) | copy-start | bytes 98308
  235.1 20.8 %copy-start.26 = (f32[1,16,512]{2,1,0:T(8,128)S(1)}, f32[1,16,512]{2,1,0:T(8,128)}, u32[]{:S(2)}) copy-start(f32[1,16,512]{2,1,0:T(8,128)} %copy.122) | copy-start | bytes 98308
  235.1 21.2 %copy-start.1 = (f32[1,16,512]{2,1,0:T(8,128)S(1)}, f32[1,16,512]{2,1,0:T(8,128)}, u32[]{:S(2)}) copy-start(f32[1,16,512]{2,1,0:T(8,128)} %copy.141) | copy-start | bytes 98308
  235.8 19.9 %copy-start.33 = (f32[1,16,512]{2,1,0:T(8,128)S(1)}, f32[1,16,512]{2,1,0:T(8,128)}, u32[]{:S(2)}) copy-start(f32[1,16,512]{2,1,0:T(8,128)} %copy.115) | copy-start | bytes 98308
  312.5 48.1 %collective-permute-start.1 = (f32[16,32768]{1,0:T(8,128)S(1)}, f32[16,32768]{1,0:T(8,128)S(1)}, u32[]{:S(2)}, u32[]{:S(2)}) collective-permute-start(f32[16,32768]{1,0:T(8,128)S(1)} %bitcast.160), channel_id=1, source_target_pairs={{0,128},{128,0},{1,129},{129,1},{2,130},{130,2},{3,131},{131,3},{4... | collective-permute-start | bytes 6291464 | tf_op jit(solution)/shard_map/ppermute | solution.py:10
  (7 other events, 109.2 us)
